TPU v7x, 32 devices: a whole 2x2x4 slice. The times are simulated.
32 devices in a mesh: dp: 4 (over y, x), expert: 8 (over z, core).
Axes of the slice: x: 2, y: 2, z: 4, core: 2. Of those that a mesh axis runs over, the one named last changes fastest.
Arguments:
- tokens: bfloat16 [2048, 4096], P(('dp', 'expert')), may hold values from -6 to 6
- grads_out: bfloat16 [2048, 4096], P(('dp', 'expert')), may hold values from -6 to 6
- routes: int32 [2048, 2], P(('dp', 'expert')), may hold values from 0 to 31, all different within a row; in each aligned block of 64 rows (0 to 63, 64 to 127, ...) at most 4 rows name the same one
- route_weights: float32 [2048, 2], P(('dp', 'expert')), may hold values from 0.2 to 1
- depth_filter: float32 [32, 5, 512], P('expert'), may hold values from -2.5 to 2.5
- point_weight: bfloat16 [512, 32, 1024], P('dp', 'expert'), may hold values from -0.25 to 0.25
Outputs:
- mixed: bfloat16 [2048, 4096], P(('dp', 'expert'))
- token_grads: bfloat16 [2048, 4096], P(('dp', 'expert'))
- point_grads: float32 [512, 32, 1024], P('dp', 'expert')
- depth_grads: float32 [32, 5, 512], P('expert')
Inputs may be any that keep to these rules, and one draw needn't show every extreme that they name: `routes`: the two experts of a frame differ; among the 64 frames of one device no expert is named more than 4 times.
All inputs are finite; a program needn't handle non-finite values.
Results may differ from a plain program's by a relative error of at most 0.0095.
Values may be sent and summed in bfloat16 or wider, within the bound.
No kernel may reach another device: no remote copies, remote signals or barrier semaphores. Data moves between devices by JAX's collectives and lax.ppermute only.
A program may use at most 64 MiB of HBM per device.

v0:
```python
import jax
import jax.numpy as jnp
from jax import lax
from jax.sharding import PartitionSpec as P

KERNEL_TAPS = 5
DILATION_STEP = 2
CAP = 4


def shifted_input(field, tap_offset):
    width = field.shape[-2]
    pads = [(0, 0)] * (field.ndim - 2) + [(abs(tap_offset), abs(tap_offset)), (0, 0)]
    padded = jnp.pad(field, pads)
    begin = abs(tap_offset) + tap_offset
    return lax.slice_in_dim(padded, begin, begin + width, axis=field.ndim - 2)


def shards(tokens, grads_out, routes, route_weights, depth_filter, point_weight):
    tok_count = tokens.shape[0]
    dev_count = lax.axis_size("expert")
    exp_local = depth_filter.shape[0]
    exp_total = exp_local * dev_count
    slot_count = 2 * tok_count
    frame_width = tokens.shape[1]
    channels = point_weight.shape[2] // 2
    bins = frame_width // channels
    route_flat = routes.reshape(slot_count)
    onehot = (route_flat[:, None] == jnp.arange(exp_total, dtype=jnp.int32)[None, :]).astype(
        jnp.int32
    )
    ranks = jnp.sum((jnp.cumsum(onehot, axis=0) - 1) * onehot, axis=1)
    slot_ids = route_flat * CAP + ranks
    placing = (slot_ids[None, :] == jnp.arange(exp_total * CAP, dtype=jnp.int32)[:, None]).astype(
        jnp.bfloat16
    )
    tokens_twice = jnp.repeat(tokens, 2, axis=0)
    cotan_twice = (
        route_weights.reshape(slot_count, 1) * jnp.repeat(grads_out, 2, axis=0).astype(jnp.float32)
    ).astype(jnp.bfloat16)
    send_frames = jnp.dot(placing, tokens_twice, preferred_element_type=jnp.float32).astype(
        jnp.bfloat16
    )
    send_cotan = jnp.dot(placing, cotan_twice, preferred_element_type=jnp.float32).astype(
        jnp.bfloat16
    )
    send_frames = send_frames.reshape(dev_count, exp_local * CAP, frame_width)
    send_cotan = send_cotan.reshape(dev_count, exp_local * CAP, frame_width)

    def to_local(buffer):
        shaped = buffer.reshape(dev_count, exp_local, CAP, bins, channels)
        return jnp.transpose(shaped, (1, 0, 2, 3, 4)).reshape(
            exp_local, dev_count * CAP, bins, channels
        )

    def to_source(buffer):
        shaped = buffer.reshape(exp_local, dev_count, CAP, frame_width)
        return jnp.transpose(shaped, (1, 0, 2, 3)).reshape(dev_count, exp_local * CAP, frame_width)

    recv_frames, recv_cotan = (
        lax.all_to_all(send_frames, "expert", split_axis=0, concat_axis=0, tiled=True),
        lax.all_to_all(send_cotan, "expert", split_axis=0, concat_axis=0, tiled=True),
    )
    input_frames = to_local(recv_frames).astype(jnp.float32)
    hidden_state = jnp.zeros(input_frames.shape, jnp.float32)
    for tap_index in range(KERNEL_TAPS):
        hidden_state = hidden_state + depth_filter[:, tap_index][:, None, None, :] * shifted_input(
            input_frames, DILATION_STEP * (tap_index - KERNEL_TAPS // 2)
        )
    hidden_state = hidden_state.astype(jnp.bfloat16)
    full_filter = lax.all_gather(point_weight, "dp", axis=0, tiled=True)
    preact = jnp.einsum(
        "erpc,ceo->erpo", hidden_state, full_filter, preferred_element_type=jnp.float32
    )
    value_half = preact[..., :channels]
    gate_sig = jax.nn.sigmoid(preact[..., channels:])
    expert_out = (value_half * gate_sig).astype(jnp.bfloat16)
    cotan = to_local(recv_cotan).astype(jnp.float32)
    dpre = jnp.concatenate(
        [cotan * gate_sig, cotan * value_half * gate_sig * (1.0 - gate_sig)], axis=-1
    ).astype(jnp.bfloat16)
    dhidden = jnp.einsum("erpo,ceo->erpc", dpre, full_filter, preferred_element_type=jnp.float32)
    frame_grad = jnp.zeros(input_frames.shape, jnp.float32)
    tap_grads = []
    for tap_index in range(KERNEL_TAPS):
        tap_offset = DILATION_STEP * (tap_index - KERNEL_TAPS // 2)
        frame_grad = frame_grad + depth_filter[:, tap_index][:, None, None, :] * shifted_input(
            dhidden, -tap_offset
        )
        tap_grads.append(jnp.sum(dhidden * shifted_input(input_frames, tap_offset), axis=(1, 2)))
    frame_grad = frame_grad.astype(jnp.bfloat16)
    depth_grads = lax.psum(jnp.stack(tap_grads, axis=1).astype(jnp.bfloat16), "dp").astype(
        jnp.float32
    )
    point_grads = lax.psum_scatter(
        jnp.einsum("erpc,erpo->ceo", hidden_state, dpre, preferred_element_type=jnp.float32).astype(
            jnp.bfloat16
        ),
        "dp",
        scatter_dimension=0,
        tiled=True,
    ).astype(jnp.float32)
    back_out, back_grad = (
        lax.all_to_all(to_source(expert_out), "expert", split_axis=0, concat_axis=0, tiled=True),
        lax.all_to_all(to_source(frame_grad), "expert", split_axis=0, concat_axis=0, tiled=True),
    )
    back_out = back_out.reshape(exp_total * CAP, frame_width)
    back_grad = back_grad.reshape(exp_total * CAP, frame_width)
    slot_out = jnp.dot(placing.T, back_out, preferred_element_type=jnp.float32).reshape(
        tok_count, 2, frame_width
    )
    slot_grad = jnp.dot(placing.T, back_grad, preferred_element_type=jnp.float32).reshape(
        tok_count, 2, frame_width
    )
    mixed = jnp.sum(route_weights[:, :, None] * slot_out, axis=1).astype(jnp.bfloat16)
    token_grads = jnp.sum(slot_grad, axis=1).astype(jnp.bfloat16)
    return (mixed, token_grads, point_grads, depth_grads)


def solution(mesh):
    placed = (
        P(("dp", "expert"), None),
        P(("dp", "expert"), None),
        P(("dp", "expert"), None),
        P(("dp", "expert"), None),
        P("expert", None, None),
        P("dp", "expert", None),
    )
    return jax.shard_map(
        shards,
        mesh=mesh,
        in_specs=placed,
        out_specs=(
            P(("dp", "expert"), None),
            P(("dp", "expert"), None),
            P("dp", "expert", None),
            P("expert", None, None),
        ),
        check_vma=False,
    )
```

profile of v0, /device:TPU:0, one launch (start us, length us, event | category | flops | bytes accessed | tf_op | source)
XLA Modules:
  0.0 179.3 jit_solution(13614706876543647294)
XLA Ops:
  7.2 0.0 copy-start.8
  7.2 0.0 copy-start.5
  7.2 0.0 all-gather.2.cloned.1.call-start
  7.2 2.6 %copy.51 = bf16[128,4,1024]{2,0,1:T(8,128)(2,1)} copy(bf16[128,4,1024]{2,1,0:T(4,128)(2,1)} %param.11) | data formatting | bytes 2097152 | tf_op args[5]
  9.8 0.0 all-gather.2.cloned.1.call-update
  9.8 0.0 copy-done.8
  9.8 0.1 copy.48
  9.9 0.1 reshape.94
  10.1 0.0 copy-done.5
  10.1 1.0 broadcast_in_dim.4
  11.1 0.4 reshape.95
  11.5 0.1 fusion.18
  11.6 0.2 reduce_window_sum.11
  11.8 0.2 select_reduce_fusion
  12.0 1.4 convolution_convert_fusion.1
  13.4 6.3 %all-to-all-start = ((bf16[8,16,4096]{2,1,0:T(8,128)(2,1)}), bf16[8,16,4096]{2,1,0:T(8,128)(2,1)S(1)}, u32[]{:S(2)}, u32[]{:S(2)}) async-start(bf16[8,16,4096]{2,1,0:T(8,128)(2,1)} %bitcast.2), calls=%async_computation | async-start | bytes 2097152 | tf_op jit(solution)/shard_map/all_to_all | solution.py:61
  19.8 2.1 %broadcast_in_dim.5 = f32[64,2,4096]{2,1,0:T(2,128)S(1)} broadcast(bf16[64,4096]{1,0:T(8,128)(2,1)} %param.7), dimensions={0,2} | broadcast | bytes 2621440 | tf_op jit(solution)/shard_map/broadcast_in_dim | solution.py:39
  21.9 0.0 copy-start.7
  21.9 2.4 %convert_element_type.97 = f32[128,4096]{1,0:T(8,128)} reshape(f32[64,2,4096]{2,1,0:T(2,128)S(1)} %broadcast_in_dim.5) | data formatting | bytes 4194304 | tf_op jit(solution)/shard_map/convert_element_type | solution.py:39
  24.3 0.1 copy.54
  24.4 0.1 mul.169
  24.6 0.0 copy-start.6
  24.6 3.1 %convolution_convert_fusion = bf16[128,4096]{1,0:T(8,128)(2,1)} fusion(f32[128,4096]{1,0:T(8,128)} %convert_element_type.97, f32[128]{0:T(128)S(1)} %mul.169, s32[128]{0:T(128)S(1)} %multiply_add_fusion.1), kind=kOutput, calls=%fused_computation.10 | convolution fusion | flops 135806976 | bytes 3146752 | tf_op jit(solution)/shard_map/dot_general | solution.py:44
  27.7 18.6 %all-to-all-done = bf16[8,16,4096]{2,1,0:T(8,128)(2,1)S(1)} async-done(((bf16[8,16,4096]{2,1,0:T(8,128)(2,1)}), bf16[8,16,4096]{2,1,0:T(8,128)(2,1)S(1)}, u32[]{:S(2)}, u32[]{:S(2)}) %all-to-all-start) | async-done | bytes 1048608 | tf_op jit(solution)/shard_map/all_to_all | solution.py:61
  46.3 4.2 %all-to-all-start.2 = ((bf16[8,16,4096]{2,1,0:T(8,128)(2,1)}), bf16[8,16,4096]{2,1,0:T(8,128)(2,1)}, u32[]{:S(2)}, u32[]{:S(2)}) async-start(bf16[8,16,4096]{2,1,0:T(8,128)(2,1)} %bitcast.16), calls=%async_computation.2 | async-start | bytes 2097152 | tf_op jit(solution)/shard_map/all_to_all | solution.py:62
  50.6 0.2 reduce-scatter.4.cloned.1.call-start
  50.8 0.0 copy-done.6
  50.8 0.4 copy.65
  51.3 0.2 copy.50
  51.5 25.7 %all-to-all-done.2 = bf16[8,16,4096]{2,1,0:T(8,128)(2,1)} async-done(((bf16[8,16,4096]{2,1,0:T(8,128)(2,1)}), bf16[8,16,4096]{2,1,0:T(8,128)(2,1)}, u32[]{:S(2)}, u32[]{:S(2)}) %all-to-all-start.2) | async-done | bytes 1048608 | tf_op jit(solution)/shard_map/all_to_all | solution.py:62
  77.2 1.6 copy.66
  78.8 1.5 copy.55
  80.3 1.2 add_convert_fusion
  81.5 0.0 all-gather.2.cloned.1.call-done
  81.6 0.0 copy-start
  81.6 3.6 %fusion.2 = f32[4,32,8,1024]{3,2,1,0:T(8,128)S(1)} fusion(bf16[4,32,8,512]{3,2,1,0:T(8,128)(2,1)S(1)} %add_convert_fusion, bf16[512,4,1024]{2,0,1:T(8,128)(2,1)} %all-gather.2.cloned.1.call-done), kind=kOutput, calls=%fused_computation.14 | convolution fusion | flops 1073741824 | bytes 9437184 | tf_op jit(solution)/shard_map/erpc,ceo->erpo/dot_general | solution.py:72
  85.2 2.1 %multiply_convert_fusion.1 = (bf16[4,32,8,512]{3,2,1,0:T(8,128)(2,1)S(1)}, bf16[4,32,8,512]{3,2,1,0:T(8,128)(2,1)S(1)}, bf16[4,32,8,512]{3,2,1,0:T(8,128)(2,1)}) fusion(f32[4,32,8,512]{3,2,1,0:T(8,128)S(1)} %bitcast.82, f32[4,32,8,1024]{3,2,1,0:T(8,128)S(1)} %fusion.2), kind=kLoop, calls=%fused_computation.36 | loop fusion | flops 6291456 | bytes 9437184 | tf_op jit(solution)/shard_map/convert.16
  87.3 3.3 %bitcast_convert_fusion = bf16[4,1024,512]{2,1,0:T(8,128)(2,1)} fusion(bf16[4,32,8,512]{3,2,1,0:T(8,128)(2,1)S(1)} %add_convert_fusion, bf16[4,32,8,512]{3,2,1,0:T(8,128)(2,1)S(1)} %get-tuple-element.26, bf16[4,32,8,512]{3,2,1,0:T(8,128)(2,1)S(1)} %get-tuple-element.25), kind=kOutput, calls=%fused_computation | convolution fusion | flops 1080033280 | bytes 7340032 | tf_op jit(solution)/shard_map/erpc,erpo->ceo/dot_general | solution.py:96
  90.6 0.0 copy-done.2
  90.6 6.5 %copy.63 = bf16[512,4096]{1,0:T(8,128)(2,1)} copy(bf16[512,4096]{0,1:T(8,128)(2,1)} %bitcast.85) | data formatting | bytes 8388608
  97.1 0.0 reduce-scatter.4.cloned.1.call-update
  97.1 1.2 copy-done.3
  98.3 3.8 %fusion = f32[4,32,8,512]{3,2,1,0:T(8,128)S(1)} fusion(bf16[512,4,1024]{2,0,1:T(8,128)(2,1)} %all-gather.2.cloned.1.call-done, bf16[4,32,8,512]{3,2,1,0:T(8,128)(2,1)} %copy-done.4, bf16[4,32,8,512]{3,2,1,0:T(8,128)(2,1)S(1)} %copy-done.3), kind=kOutput, calls=%fused_computation.12 | convolution fusion | flops 1077936128 | bytes 8388608 | tf_op jit(solution)/shard_map/erpo,ceo->erpc/dot_general | solution.py:82
  102.1 2.5 %multiply_reduce_fusion = (bf16[4,512]{1,0:T(4,128)(2,1)S(1)}, bf16[4,512]{1,0:T(4,128)(2,1)S(1)}, bf16[4,512]{1,0:T(4,128)(2,1)S(1)}, bf16[4,512]{1,0:T(4,128)(...) fusion(f32[4,32,8,512]{3,2,1,0:T(8,128)S(1)} %fusion, f32[4,32,8,512]{3,2,1,0:T(8,128)S(1)} %bitcast.79, ...), kind=kLoop, calls=%fused_computation.30 | loop fusion | flops 10475520 | bytes 5304320 | tf_op jit(solution)/shard_map/reduce_sum | solution.py:90
  104.7 0.8 reshape.101
  105.5 0.6 copy.56
  106.0 0.0 copy-start.1
  106.1 1.6 copy.57
  107.6 3.8 %all-to-all-start.3 = ((bf16[8,16,4096]{2,1,0:T(8,128)(2,1)}), bf16[8,16,4096]{2,1,0:T(8,128)(2,1)S(1)}, u32[]{:S(2)}, u32[]{:S(2)}) async-start(bf16[8,16,4096]{2,1,0:T(8,128)(2,1)} %copy.57), calls=%async_computation.3 | async-start | bytes 2097152 | tf_op jit(solution)/shard_map/all_to_all | solution.py:105
  111.4 0.0 copy-done.1
  111.4 0.8 reshape.97
  112.2 0.6 copy.52
  112.8 1.6 copy.53
  114.4 23.3 %all-to-all-done.3 = bf16[8,16,4096]{2,1,0:T(8,128)(2,1)S(1)} async-done(((bf16[8,16,4096]{2,1,0:T(8,128)(2,1)}), bf16[8,16,4096]{2,1,0:T(8,128)(2,1)S(1)}, u32[]{:S(2)}, u32[]{:S(2)}) %all-to-all-start.3) | async-done | bytes 1048608 | tf_op jit(solution)/shard_map/all_to_all | solution.py:105
  137.7 3.6 %all-to-all-start.1 = ((bf16[8,16,4096]{2,1,0:T(8,128)(2,1)}), bf16[8,16,4096]{2,1,0:T(8,128)(2,1)S(1)}, u32[]{:S(2)}, u32[]{:S(2)}) async-start(bf16[8,16,4096]{2,1,0:T(8,128)(2,1)} %copy.53), calls=%async_computation.1 | async-start | bytes 2097152 | tf_op jit(solution)/shard_map/all_to_all | solution.py:104
  141.3 0.1 reduce_sum.75
  141.4 0.1 copy.49
  141.6 16.2 %psum.7 = bf16[4,5,512]{2,0,1:T(4,128)(2,1)S(1)} all-reduce(bf16[4,5,512]{2,0,1:T(4,128)(2,1)S(1)} %constant_dynamic-update-slice_fusion), channel_id=1, replica_groups=mesh['dp'=4,'expert'=8] {'dp'}, use_global_device_ids=true, to_apply=%region_10.11 | all-reduce | flops 10240 | bytes 40960 | tf_op jit(solution)/shard_map/psum | solution.py:92
  157.8 0.6 convert_element_type.109
  158.4 1.3 convolution_reduce_fusion
  159.7 8.1 %all-to-all-done.1 = bf16[8,16,4096]{2,1,0:T(8,128)(2,1)S(1)} async-done(((bf16[8,16,4096]{2,1,0:T(8,128)(2,1)}), bf16[8,16,4096]{2,1,0:T(8,128)(2,1)S(1)}, u32[]{:S(2)}, u32[]{:S(2)}) %all-to-all-start.1) | async-done | bytes 1048608 | tf_op jit(solution)/shard_map/all_to_all | solution.py:104
  167.8 1.3 fusion.16
  169.1 1.6 copy.64
  170.7 1.8 copy.58
  (15 shorter events, 0.1 us)
Async XLA Ops:
  7.2 2.7 %copy-start.8 = (s32[64,2]{0,1:T(2,128)S(1)}, s32[64,2]{0,1:T(2,128)}, u32[]{:S(2)}) copy-start(s32[64,2]{0,1:T(2,128)} %param.8) | copy-start | bytes 1540
  7.2 2.9 %copy-start.5 = (bf16[64,4096]{1,0:T(8,128)(2,1)S(1)}, bf16[64,4096]{1,0:T(8,128)(2,1)}, u32[]{:S(2)}) copy-start(bf16[64,4096]{1,0:T(8,128)(2,1)} %param.6) | copy-start | bytes 1572868
  7.2 74.4 %all-gather.2.cloned.1.call-start = ((), (), s32[]{:S(2)}) async-start(), calls=%async_computation.5 | async-start | bytes 5242880 | tf_op jit(solution)/shard_map/all_gather | solution.py:71
  13.4 32.9 %all-to-all-start = ((bf16[8,16,4096]{2,1,0:T(8,128)(2,1)}), bf16[8,16,4096]{2,1,0:T(8,128)(2,1)S(1)}, u32[]{:S(2)}, u32[]{:S(2)}) async-start(bf16[8,16,4096]{2,1,0:T(8,128)(2,1)} %bitcast.2), calls=%async_computation | async-start | bytes 2097152 | tf_op jit(solution)/shard_map/all_to_all | solution.py:61
  21.9 2.5 %copy-start.7 = (f32[64,2]{0,1:T(2,128)S(1)}, f32[64,2]{0,1:T(2,128)}, u32[]{:S(2)}) copy-start(f32[64,2]{0,1:T(2,128)} %param.9) | copy-start | bytes 1540
  24.6 26.2 %copy-start.6 = (f32[4,5,512]{2,0,1:T(4,128)S(1)}, f32[4,5,512]{2,0,1:T(4,128)}, u32[]{:S(2)}) copy-start(f32[4,5,512]{2,0,1:T(4,128)} %param.10) | copy-start | bytes 122884
  46.3 30.8 %all-to-all-start.2 = ((bf16[8,16,4096]{2,1,0:T(8,128)(2,1)}), bf16[8,16,4096]{2,1,0:T(8,128)(2,1)}, u32[]{:S(2)}, u32[]{:S(2)}) async-start(bf16[8,16,4096]{2,1,0:T(8,128)(2,1)} %bitcast.16), calls=%async_computation.2 | async-start | bytes 2097152 | tf_op jit(solution)/shard_map/all_to_all | solution.py:62
  50.6 118.5 %reduce-scatter.4.cloned.1.call-start = ((), (), s32[]{:S(2)}) async-start(), calls=%async_computation.6 | async-start | bytes 5242880
  81.6 3.6 %copy-start = (f32[4,8,4,8,512]{4,3,2,1,0:T(8,128)S(1)}, f32[4,8,4,8,512]{4,3,2,1,0:T(8,128)}, u32[]{:S(2)}) copy-start(f32[4,8,4,8,512]{4,3,2,1,0:T(8,128)} %copy.55) | copy-start | bytes 6291460
  87.3 3.3 %copy-start.2 = (bf16[4,32,8,512]{3,2,1,0:T(8,128)(2,1)}, bf16[4,32,8,512]{3,2,1,0:T(8,128)(2,1)S(1)}, u32[]{:S(2)}) copy-start(bf16[4,32,8,512]{3,2,1,0:T(8,128)(2,1)S(1)} %get-tuple-element.25) | copy-start | bytes 3145732
  87.3 3.3 %copy-start.4 = (bf16[4,32,8,512]{3,2,1,0:T(8,128)(2,1)}, bf16[4,32,8,512]{3,2,1,0:T(8,128)(2,1)S(1)}, u32[]{:S(2)}) copy-start(bf16[4,32,8,512]{3,2,1,0:T(8,128)(2,1)S(1)} %get-tuple-element.26) | copy-start | bytes 3145732
  97.1 1.2 copy-start.3
  106.0 5.4 %copy-start.1 = (bf16[4,32,8,512]{3,2,1,0:T(8,128)(2,1)S(1)}, bf16[4,32,8,512]{3,2,1,0:T(8,128)(2,1)}, u32[]{:S(2)}) copy-start(bf16[4,32,8,512]{3,2,1,0:T(8,128)(2,1)} %get-tuple-element.27) | copy-start | bytes 3145732
  107.6 30.1 %all-to-all-start.3 = ((bf16[8,16,4096]{2,1,0:T(8,128)(2,1)}), bf16[8,16,4096]{2,1,0:T(8,128)(2,1)S(1)}, u32[]{:S(2)}, u32[]{:S(2)}) async-start(bf16[8,16,4096]{2,1,0:T(8,128)(2,1)} %copy.57), calls=%async_computation.3 | async-start | bytes 2097152 | tf_op jit(solution)/shard_map/all_to_all | solution.py:105
  137.7 30.1 %all-to-all-start.1 = ((bf16[8,16,4096]{2,1,0:T(8,128)(2,1)}), bf16[8,16,4096]{2,1,0:T(8,128)(2,1)S(1)}, u32[]{:S(2)}, u32[]{:S(2)}) async-start(bf16[8,16,4096]{2,1,0:T(8,128)(2,1)} %copy.53), calls=%async_computation.1 | async-start | bytes 2097152 | tf_op jit(solution)/shard_map/all_to_all | solution.py:104
Sparse Core Ops, SparseCore 0:
  9.9 55.3 all-gather.1
  97.2 51.7 reduce-scatter.3
where the time goes:
time: 180 us; the launch traced here: 179 us
  waiting for transfers between devices  75.8 us (42%)
  local copies, waits for them, and re-layouts  30.1 us (17%)
  starting transfers between devices  18.2 us (10%)
  matrix products  17.8 us (10%)
  blocking collectives  16.2 us (9%)
  between operations  14.3 us (8%)
  other arithmetic  6.93 us (4%)
    all_to_all x1, waiting for transfers between devices, shards(): lax.all_to_all(send_cotan, 'expert', split_axis=0, concat_axis=0, tiled=T...  25.7 us
    all_to_all x1, waiting for transfers between devices, shards(): lax.all_to_all(to_source(frame_grad), 'expert', split_axis=0, concat_axis...  23.3 us
    all_to_all x1, waiting for transfers between devices, shards(): lax.all_to_all(send_frames, 'expert', split_axis=0, concat_axis=0, tiled=...  18.6 us
    psum x1, blocking collectives, shards(): lax.psum(jnp.stack(tap_grads, axis=1).astype(jnp.bfloat16), 'dp')  16.2 us
    unnamed x30, local copies, waits for them, and re-layouts  15.9 us
    all_to_all x1, waiting for transfers between devices, shards(): lax.all_to_all(to_source(expert_out), 'expert', split_axis=0, concat_axis...  8.08 us
    all_to_all x1, starting transfers between devices, shards(): lax.all_to_all(send_frames, 'expert', split_axis=0, concat_axis=0, tiled=...  6.33 us
    all_to_all x1, starting transfers between devices, shards(): lax.all_to_all(send_cotan, 'expert', split_axis=0, concat_axis=0, tiled=T...  4.24 us
  transfers between devices with their start and end apart: 6, of which 4 were waited for; matrix products, arithmetic and copies ran while one was open for 18% of the time, Pallas kernels for 0%

commit v1 on v0

--- a/solution.py
+++ b/solution.py
@@ -6,6 +6,38 @@
 KERNEL_TAPS = 5
 DILATION_STEP = 2
 CAP = 4
+
+
+def pack_region(panel, dim_at, matrix):
+    spare = panel.shape
+    state_now = panel.reshape(
+        *spare[:dim_at], matrix, spare[dim_at] // matrix, *spare[dim_at + 1 :]
+    )
+    return jnp.moveaxis(state_now, dim_at, 0)
+
+
+def deliver_panel(q_in, dimension_no):
+    r1 = list(q_in.shape[1:])
+    r1[dimension_no] *= q_in.shape[0]
+    return jnp.moveaxis(q_in, 0, dimension_no).reshape(r1)
+
+
+def _place_blocks(dev_axis, payload, inner_x, piece_in):
+    found_now = lax.axis_size(dev_axis)
+    after = lax.axis_index(dev_axis)
+    m_next, f_now = (found_now, after)
+    met_up = pack_region(piece_in, payload, m_next)
+    built = met_up
+    k0 = 1
+    while k0 < m_next:
+        z, low = ((f_now + k0) % m_next, (f_now - k0) % m_next)
+        base_arr = lax.dynamic_index_in_dim(met_up, z, 0)
+        finding = lax.ppermute(
+            base_arr, dev_axis, [(jj, (jj + k0) % m_next) for jj in range(m_next)]
+        )
+        built = lax.dynamic_update_slice_in_dim(built, finding, low, axis=0)
+        k0 = k0 + 1
+    return deliver_panel(built, inner_x)
 
 
 def shifted_input(field, tap_offset):
@@ -59,7 +91,7 @@
 
     recv_frames, recv_cotan = (
         lax.all_to_all(send_frames, "expert", split_axis=0, concat_axis=0, tiled=True),
-        lax.all_to_all(send_cotan, "expert", split_axis=0, concat_axis=0, tiled=True),
+        _place_blocks("expert", 0, 0, send_cotan),
     )
     input_frames = to_local(recv_frames).astype(jnp.float32)
     hidden_state = jnp.zeros(input_frames.shape, jnp.float32)

time: 180 us -> 174 us (0.967)
  waiting for transfers between devices: 75.8 us -> 63.1 us
  starting transfers between devices: 18.2 us -> 28.3 us
  local copies, waits for them, and re-layouts: 30.1 us -> 27.9 us
    ppermute x0 -> x7, waiting for transfers between devices: none -> 31.3 us  [_place_blocks(): lax.ppermute(base_arr, dev_axis, [(jj, (jj + k0) % m_next) for jj in rang...]
    all_to_all x1 -> x0, waiting for transfers between devices: 25.7 us -> none  [shards(): lax.all_to_all(send_cotan, 'expert', split_axis=0, concat_axis=0, tiled=T...]
    all_to_all x1, waiting for transfers between devices: 18.6 us -> 0.01 us  [shards(): lax.all_to_all(send_frames, 'expert', split_axis=0, concat_axis=0, tiled=...]
    ppermute x0 -> x7, starting transfers between devices: none -> 8.5 us  [_place_blocks(): lax.ppermute(base_arr, dev_axis, [(jj, (jj + k0) % m_next) for jj in rang...]
    all_to_all x1, starting transfers between devices: 3.78 us -> 9.88 us  [shards(): lax.all_to_all(to_source(frame_grad), 'expert', split_axis=0, concat_axis...]
    all_to_all x1 -> x0, starting transfers between devices: 4.24 us -> none  [shards(): lax.all_to_all(send_cotan, 'expert', split_axis=0, concat_axis=0, tiled=T...]
    unnamed x30 -> x32, local copies, waits for them, and re-layouts: 15.9 us -> 14.7 us
  transfers between devices with their start and end apart: 6 -> 12, of which waited for: 4 -> 5; matrix products, arithmetic and copies ran while one was open for 18% -> 17% of each run, Pallas kernels for 0% -> 0%
where the time goes in v1:
time: 174 us
  waiting for transfers between devices  63.1 us (36%)
  starting transfers between devices  28.3 us (16%)
  local copies, waits for them, and re-layouts  27.9 us (16%)
  matrix products  16.8 us (10%)
  blocking collectives  16.2 us (9%)
  between operations  14.6 us (8%)
  other arithmetic  6.94 us (4%)
    ppermute x7, waiting for transfers between devices, _place_blocks(): lax.ppermute(base_arr, dev_axis, [(jj, (jj + k0) % m_next) for jj in rang...  31.3 us
    all_to_all x1, waiting for transfers between devices, shards(): lax.all_to_all(to_source(frame_grad), 'expert', split_axis=0, concat_axis...  23.6 us
    psum x1, blocking collectives, shards(): lax.psum(jnp.stack(tap_grads, axis=1).astype(jnp.bfloat16), 'dp')  16.2 us
    unnamed x32, local copies, waits for them, and re-layouts  14.7 us
    all_to_all x1, starting transfers between devices, shards(): lax.all_to_all(to_source(frame_grad), 'expert', split_axis=0, concat_axis...  9.88 us
    ppermute x7, starting transfers between devices, _place_blocks(): lax.ppermute(base_arr, dev_axis, [(jj, (jj + k0) % m_next) for jj in rang...  8.5 us
    all_to_all x1, waiting for transfers between devices, shards(): lax.all_to_all(to_source(expert_out), 'expert', split_axis=0, concat_axis...  8.06 us
    all_to_all x1, starting transfers between devices, shards(): lax.all_to_all(send_frames, 'expert', split_axis=0, concat_axis=0, tiled=...  6.29 us
  transfers between devices with their start and end apart: 12, of which 5 were waited for; matrix products, arithmetic and copies ran while one was open for 17% of the time, Pallas kernels for 0%

profile of v1, /device:TPU:0, one launch (start us, length us, event | category | flops | bytes accessed | tf_op | source)
XLA Modules:
  0.0 173.9 jit_solution(7581808371855673329)
XLA Ops:
  7.2 0.0 all-gather.2.cloned.1.call-start
  7.2 2.6 %copy.51 = bf16[128,4,1024]{2,0,1:T(8,128)(2,1)} copy(bf16[128,4,1024]{2,1,0:T(4,128)(2,1)} %param.11) | data formatting | bytes 2097152 | tf_op args[5]
  9.8 0.0 all-gather.2.cloned.1.call-update
  9.8 0.1 copy.48
  9.9 0.1 reshape.90
  10.1 0.1 fusion.18
  10.2 0.2 reduce_window_sum.11
  10.3 1.0 broadcast_in_dim.5
  11.4 0.0 copy-start.8
  11.4 2.4 %convert_element_type.97 = f32[128,4096]{1,0:T(8,128)} reshape(f32[64,2,4096]{2,1,0:T(2,128)S(1)} %broadcast_in_dim.5) | data formatting | bytes 4194304 | tf_op jit(solution)/shard_map/convert_element_type | solution.py:71
  13.8 0.1 copy.54
  13.9 0.1 mul.169
  14.1 0.2 select_reduce_fusion
  14.3 2.1 %convolution_convert_fusion = bf16[128,4096]{1,0:T(8,128)(2,1)S(1)} fusion(f32[128,4096]{1,0:T(8,128)} %convert_element_type.97, f32[128]{0:T(128)S(1)} %mul.169, s32[128]{0:T(128)S(1)} %multiply_add_fusion.1), kind=kOutput, calls=%fused_computation.10 | convolution fusion | flops 135806976 | bytes 3146752 | tf_op jit(solution)/shard_map/dot_general | solution.py:76
  16.4 0.5 collective-permute-start
  16.9 1.0 broadcast_in_dim.4
  17.9 0.4 reshape.91
  18.3 1.4 convolution_convert_fusion.1
  19.8 6.3 %all-to-all-start = ((bf16[8,16,4096]{2,1,0:T(8,128)(2,1)}), bf16[8,16,4096]{2,1,0:T(8,128)(2,1)S(1)}, u32[]{:S(2)}, u32[]{:S(2)}) async-start(bf16[8,16,4096]{2,1,0:T(8,128)(2,1)} %bitcast.2), calls=%async_computation | async-start | bytes 2097152 | tf_op jit(solution)/shard_map/all_to_all | solution.py:93
  26.1 0.0 reduce-scatter.4.cloned.1.call-start
  26.4 0.1 constant_dynamic-slice_fusion
  26.4 1.8 %collective-permute-start.1 = (bf16[1,1,16,4096]{3,2,0,1:T(8,128)(2,1)S(1)}, bf16[1,1,16,4096]{3,2,0,1:T(8,128)(2,1)S(1)}, u32[]{:S(2)}, u32[]{:S(2)}) collective-permute-start(bf16[1,1,16,4096]{3,2,0,1:T(8,128)(2,1)S(1)} %get-tuple-element.34), channel_id=1, source_target_pairs={{0,2},{1,3},{2,4},{3,5},{4,6},{5,7},{6,0},{7,1},{8,10},{9,11},{10,... | collective-permute-start | bytes 393224 | tf_op jit(solution)/shard_map/ppermute | solution.py:35
  28.3 0.9 collective-permute-start.2
  29.2 1.5 collective-permute-start.3
  30.7 2.3 %collective-permute-start.4 = (bf16[1,1,16,4096]{3,2,0,1:T(8,128)(2,1)S(1)}, bf16[1,1,16,4096]{3,2,0,1:T(8,128)(2,1)S(1)}, u32[]{:S(2)}, u32[]{:S(2)}) collective-permute-start(bf16[1,1,16,4096]{3,2,0,1:T(8,128)(2,1)S(1)} %get-tuple-element.31), channel_id=1, source_target_pairs={{0,5},{1,6},{2,7},{3,0},{4,1},{5,2},{6,3},{7,4},{8,13},{9,14},{10,... | collective-permute-start | bytes 393224 | tf_op jit(solution)/shard_map/ppermute | solution.py:35
  33.0 1.5 collective-permute-start.5
  34.4 16.9 %collective-permute-done.1 = bf16[1,1,16,4096]{3,2,0,1:T(8,128)(2,1)S(1)} collective-permute-done((bf16[1,1,16,4096]{3,2,0,1:T(8,128)(2,1)S(1)}, bf16[1,1,16,4096]{3,2,0,1:T(8,128)(2,1)S(1)}, u32[]{:S(2)}, u32[]{:S(2)}) %collective-permute-start.1) | collective-permute-done | bytes 131104 | tf_op jit(solution)/shard_map/ppermute | solution.py:35
  51.4 0.0 collective-permute-start.6
  51.4 13.4 %collective-permute-done.2 = bf16[1,1,16,4096]{3,2,0,1:T(8,128)(2,1)S(1)} collective-permute-done((bf16[1,1,16,4096]{3,2,0,1:T(8,128)(2,1)S(1)}, bf16[1,1,16,4096]{3,2,0,1:T(8,128)(2,1)S(1)}, u32[]{:S(2)}, u32[]{:S(2)}) %collective-permute-start.2) | collective-permute-done | bytes 131104 | tf_op jit(solution)/shard_map/ppermute | solution.py:35
  64.8 0.9 collective-permute-done.3
  65.9 0.4 copy.66
  66.3 1.5 copy.55
  67.8 0.4 copy.65
  68.3 0.2 copy.50
  68.5 1.2 add_convert_fusion
  69.7 0.0 all-gather.2.cloned.1.call-done
  69.7 0.0 copy-start
  69.7 3.6 %fusion.2 = f32[4,32,8,1024]{3,2,1,0:T(8,128)S(1)} fusion(bf16[4,32,8,512]{3,2,1,0:T(8,128)(2,1)S(1)} %add_convert_fusion, bf16[512,4,1024]{2,0,1:T(8,128)(2,1)} %all-gather.2.cloned.1.call-done), kind=kOutput, calls=%fused_computation.14 | convolution fusion | flops 1073741824 | bytes 9437184 | tf_op jit(solution)/shard_map/erpc,ceo->erpo/dot_general | solution.py:104
  73.3 2.1 %multiply_convert_fusion.1 = (bf16[4,32,8,512]{3,2,1,0:T(8,128)(2,1)S(1)}, bf16[4,32,8,512]{3,2,1,0:T(8,128)(2,1)S(1)}, bf16[4,32,8,512]{3,2,1,0:T(8,128)(2,1)}) fusion(f32[4,32,8,512]{3,2,1,0:T(8,128)S(1)} %bitcast.87, f32[4,32,8,1024]{3,2,1,0:T(8,128)S(1)} %fusion.2), kind=kLoop, calls=%fused_computation.36 | loop fusion | flops 6291456 | bytes 9437184 | tf_op jit(solution)/shard_map/convert.16
  75.5 3.3 %bitcast_convert_fusion = bf16[4,1024,512]{2,1,0:T(8,128)(2,1)} fusion(bf16[4,32,8,512]{3,2,1,0:T(8,128)(2,1)S(1)} %add_convert_fusion, bf16[4,32,8,512]{3,2,1,0:T(8,128)(2,1)S(1)} %get-tuple-element.26, bf16[4,32,8,512]{3,2,1,0:T(8,128)(2,1)S(1)} %get-tuple-element.25), kind=kOutput, calls=%fused_computation | convolution fusion | flops 1080033280 | bytes 7340032 | tf_op jit(solution)/shard_map/erpc,erpo->ceo/dot_general | solution.py:128
  78.7 6.5 %copy.63 = bf16[512,4096]{1,0:T(8,128)(2,1)} copy(bf16[512,4096]{0,1:T(8,128)(2,1)} %bitcast.90) | data formatting | bytes 8388608
  85.2 0.0 reduce-scatter.4.cloned.1.call-update
  85.2 1.2 copy-done.3
  86.4 3.8 %fusion = f32[4,32,8,512]{3,2,1,0:T(8,128)S(1)} fusion(bf16[512,4,1024]{2,0,1:T(8,128)(2,1)} %all-gather.2.cloned.1.call-done, bf16[4,32,8,512]{3,2,1,0:T(8,128)(2,1)} %copy-done.4, bf16[4,32,8,512]{3,2,1,0:T(8,128)(2,1)S(1)} %copy-done.3), kind=kOutput, calls=%fused_computation.12 | convolution fusion | flops 1077936128 | bytes 8388608 | tf_op jit(solution)/shard_map/erpo,ceo->erpc/dot_general | solution.py:114
  90.2 2.5 %multiply_reduce_fusion = (bf16[4,512]{1,0:T(4,128)(2,1)S(1)}, bf16[4,512]{1,0:T(4,128)(2,1)S(1)}, bf16[4,512]{1,0:T(4,128)(2,1)S(1)}, bf16[4,512]{1,0:T(4,128)(...) fusion(f32[4,32,8,512]{3,2,1,0:T(8,128)S(1)} %fusion, f32[4,32,8,512]{3,2,1,0:T(8,128)S(1)} %bitcast.81, ...), kind=kLoop, calls=%fused_computation.30 | loop fusion | flops 10475520 | bytes 5304320 | tf_op jit(solution)/shard_map/reduce_sum | solution.py:122
  92.8 0.8 reshape.96
  93.6 0.6 copy.56
  94.2 0.0 copy-start.1
  94.2 1.6 copy.57
  95.8 9.9 %all-to-all-start.2 = ((bf16[8,16,4096]{2,1,0:T(8,128)(2,1)}), bf16[8,16,4096]{2,1,0:T(8,128)(2,1)S(1)}, u32[]{:S(2)}, u32[]{:S(2)}) async-start(bf16[8,16,4096]{2,1,0:T(8,128)(2,1)} %copy.57), calls=%async_computation.2 | async-start | bytes 2097152 | tf_op jit(solution)/shard_map/all_to_all | solution.py:137
  105.7 0.8 reshape.93
  106.5 0.6 copy.52
  107.1 1.6 copy.53
  108.6 23.6 %all-to-all-done.2 = bf16[8,16,4096]{2,1,0:T(8,128)(2,1)S(1)} async-done(((bf16[8,16,4096]{2,1,0:T(8,128)(2,1)}), bf16[8,16,4096]{2,1,0:T(8,128)(2,1)S(1)}, u32[]{:S(2)}, u32[]{:S(2)}) %all-to-all-start.2) | async-done | bytes 1048608 | tf_op jit(solution)/shard_map/all_to_all | solution.py:137
  132.2 3.6 %all-to-all-start.1 = ((bf16[8,16,4096]{2,1,0:T(8,128)(2,1)}), bf16[8,16,4096]{2,1,0:T(8,128)(2,1)S(1)}, u32[]{:S(2)}, u32[]{:S(2)}) async-start(bf16[8,16,4096]{2,1,0:T(8,128)(2,1)} %copy.53), calls=%async_computation.1 | async-start | bytes 2097152 | tf_op jit(solution)/shard_map/all_to_all | solution.py:136
  135.8 0.1 reduce_sum.75
  136.0 0.1 copy.49
  136.1 16.2 %psum.7 = bf16[4,5,512]{2,0,1:T(4,128)(2,1)S(1)} all-reduce(bf16[4,5,512]{2,0,1:T(4,128)(2,1)S(1)} %constant_dynamic-update-slice_fusion), channel_id=1, replica_groups=mesh['dp'=4,'expert'=8] {'dp'}, use_global_device_ids=true, to_apply=%region_10.11 | all-reduce | flops 10240 | bytes 40960 | tf_op jit(solution)/shard_map/psum | solution.py:124
  152.3 0.6 convert_element_type.109
  153.0 1.3 convolution_reduce_fusion
  154.3 8.1 %all-to-all-done.1 = bf16[8,16,4096]{2,1,0:T(8,128)(2,1)S(1)} async-done(((bf16[8,16,4096]{2,1,0:T(8,128)(2,1)}), bf16[8,16,4096]{2,1,0:T(8,128)(2,1)S(1)}, u32[]{:S(2)}, u32[]{:S(2)}) %all-to-all-start.1) | async-done | bytes 1048608 | tf_op jit(solution)/shard_map/all_to_all | solution.py:136
  162.3 1.3 fusion.16
  163.6 1.6 copy.64
  165.3 1.8 %copy.58 = f32[128,4,1024]{2,1,0:T(4,128)} copy(bf16[128,4,1024]{0,2,1:T(8,128)(2,1)S(1)} %bitcast.89) | data formatting | bytes 3145728
  (37 shorter events, 0.2 us)
Async XLA Ops:
  7.2 2.7 %copy-start.9 = (s32[64,2]{0,1:T(2,128)S(1)}, s32[64,2]{0,1:T(2,128)}, u32[]{:S(2)}) copy-start(s32[64,2]{0,1:T(2,128)} %param.8) | copy-start | bytes 1540
  7.2 3.2 %copy-start.5 = (bf16[64,4096]{1,0:T(8,128)(2,1)S(1)}, bf16[64,4096]{1,0:T(8,128)(2,1)}, u32[]{:S(2)}) copy-start(bf16[64,4096]{1,0:T(8,128)(2,1)} %param.7) | copy-start | bytes 1572868
  7.2 62.5 %all-gather.2.cloned.1.call-start = ((), (), s32[]{:S(2)}) async-start(), calls=%async_computation.4 | async-start | bytes 5242880 | tf_op jit(solution)/shard_map/all_gather | solution.py:103
  11.4 2.5 %copy-start.8 = (f32[64,2]{0,1:T(2,128)S(1)}, f32[64,2]{0,1:T(2,128)}, u32[]{:S(2)}) copy-start(f32[64,2]{0,1:T(2,128)} %param.9) | copy-start | bytes 1540
  13.8 3.1 %copy-start.6 = (bf16[64,4096]{1,0:T(8,128)(2,1)S(1)}, bf16[64,4096]{1,0:T(8,128)(2,1)}, u32[]{:S(2)}) copy-start(bf16[64,4096]{1,0:T(8,128)(2,1)} %param.6) | copy-start | bytes 1572868
  16.4 10.0 %collective-permute-start = (bf16[1,1,16,4096]{3,2,0,1:T(8,128)(2,1)S(1)}, bf16[1,1,16,4096]{3,2,0,1:T(8,128)(2,1)S(1)}, u32[]{:S(2)}, u32[]{:S(2)}) collective-permute-start(bf16[1,1,16,4096]{3,2,0,1:T(8,128)(2,1)S(1)} %constant_dynamic-slice_fusion.6), channel_id=1, source_target_pairs={{0,1},{1,2},{2,3},{3,4},{4,5},{5,6},{6,7},{7,0},{8,9},{9,10},{10,1... | collective-permute-start | bytes 393224 | tf_op jit(solution)/shard_map/ppermute | solution.py:35
  19.8 8.5 %copy-start.7 = (f32[4,5,512]{2,0,1:T(4,128)S(1)}, f32[4,5,512]{2,0,1:T(4,128)}, u32[]{:S(2)}) copy-start(f32[4,5,512]{2,0,1:T(4,128)} %param.10) | copy-start | bytes 122884
  19.8 48.1 %all-to-all-start = ((bf16[8,16,4096]{2,1,0:T(8,128)(2,1)}), bf16[8,16,4096]{2,1,0:T(8,128)(2,1)S(1)}, u32[]{:S(2)}, u32[]{:S(2)}) async-start(bf16[8,16,4096]{2,1,0:T(8,128)(2,1)} %bitcast.2), calls=%async_computation | async-start | bytes 2097152 | tf_op jit(solution)/shard_map/all_to_all | solution.py:93
  26.1 137.6 %reduce-scatter.4.cloned.1.call-start = ((), (), s32[]{:S(2)}) async-start(), calls=%async_computation.5 | async-start | bytes 5242880
  26.4 24.9 %collective-permute-start.1 = (bf16[1,1,16,4096]{3,2,0,1:T(8,128)(2,1)S(1)}, bf16[1,1,16,4096]{3,2,0,1:T(8,128)(2,1)S(1)}, u32[]{:S(2)}, u32[]{:S(2)}) collective-permute-start(bf16[1,1,16,4096]{3,2,0,1:T(8,128)(2,1)S(1)} %get-tuple-element.34), channel_id=1, source_target_pairs={{0,2},{1,3},{2,4},{3,5},{4,6},{5,7},{6,0},{7,1},{8,10},{9,11},{10,... | collective-permute-start | bytes 393224 | tf_op jit(solution)/shard_map/ppermute | solution.py:35
  28.3 36.6 %collective-permute-start.2 = (bf16[1,1,16,4096]{3,2,0,1:T(8,128)(2,1)S(1)}, bf16[1,1,16,4096]{3,2,0,1:T(8,128)(2,1)S(1)}, u32[]{:S(2)}, u32[]{:S(2)}) collective-permute-start(bf16[1,1,16,4096]{3,2,0,1:T(8,128)(2,1)S(1)} %get-tuple-element.33), channel_id=1, source_target_pairs={{0,3},{1,4},{2,5},{3,6},{4,7},{5,0},{6,1},{7,2},{8,11},{9,12},{10,... | collective-permute-start | bytes 393224 | tf_op jit(solution)/shard_map/ppermute | solution.py:35
  29.2 36.6 %collective-permute-start.3 = (bf16[1,1,16,4096]{3,2,0,1:T(8,128)(2,1)S(1)}, bf16[1,1,16,4096]{3,2,0,1:T(8,128)(2,1)S(1)}, u32[]{:S(2)}, u32[]{:S(2)}) collective-permute-start(bf16[1,1,16,4096]{3,2,0,1:T(8,128)(2,1)S(1)} %get-tuple-element.32), channel_id=1, source_target_pairs={{0,4},{1,5},{2,6},{3,7},{4,0},{5,1},{6,2},{7,3},{8,12},{9,13},{10,... | collective-permute-start | bytes 393224 | tf_op jit(solution)/shard_map/ppermute | solution.py:35
  30.7 35.1 %collective-permute-start.4 = (bf16[1,1,16,4096]{3,2,0,1:T(8,128)(2,1)S(1)}, bf16[1,1,16,4096]{3,2,0,1:T(8,128)(2,1)S(1)}, u32[]{:S(2)}, u32[]{:S(2)}) collective-permute-start(bf16[1,1,16,4096]{3,2,0,1:T(8,128)(2,1)S(1)} %get-tuple-element.31), channel_id=1, source_target_pairs={{0,5},{1,6},{2,7},{3,0},{4,1},{5,2},{6,3},{7,4},{8,13},{9,14},{10,... | collective-permute-start | bytes 393224 | tf_op jit(solution)/shard_map/ppermute | solution.py:35
  33.0 32.9 %collective-permute-start.5 = (bf16[1,1,16,4096]{3,2,0,1:T(8,128)(2,1)S(1)}, bf16[1,1,16,4096]{3,2,0,1:T(8,128)(2,1)S(1)}, u32[]{:S(2)}, u32[]{:S(2)}) collective-permute-start(bf16[1,1,16,4096]{3,2,0,1:T(8,128)(2,1)S(1)} %get-tuple-element.30), channel_id=1, source_target_pairs={{0,6},{1,7},{2,0},{3,1},{4,2},{5,3},{6,4},{7,5},{8,14},{9,15},{10,... | collective-permute-start | bytes 393224 | tf_op jit(solution)/shard_map/ppermute | solution.py:35
  51.4 14.5 %collective-permute-start.6 = (bf16[1,1,16,4096]{3,2,0,1:T(8,128)(2,1)S(1)}, bf16[1,1,16,4096]{3,2,0,1:T(8,128)(2,1)S(1)}, u32[]{:S(2)}, u32[]{:S(2)}) collective-permute-start(bf16[1,1,16,4096]{3,2,0,1:T(8,128)(2,1)S(1)} %get-tuple-element.29), channel_id=1, source_target_pairs={{0,7},{1,0},{2,1},{3,2},{4,3},{5,4},{6,5},{7,6},{8,15},{9,8},{10,9... | collective-permute-start | bytes 393224 | tf_op jit(solution)/shard_map/ppermute | solution.py:35
  69.7 3.6 %copy-start = (f32[4,8,4,8,512]{4,3,2,1,0:T(8,128)S(1)}, f32[4,8,4,8,512]{4,3,2,1,0:T(8,128)}, u32[]{:S(2)}) copy-start(f32[4,8,4,8,512]{4,3,2,1,0:T(8,128)} %copy.55) | copy-start | bytes 6291460
  75.5 3.3 %copy-start.2 = (bf16[4,32,8,512]{3,2,1,0:T(8,128)(2,1)}, bf16[4,32,8,512]{3,2,1,0:T(8,128)(2,1)S(1)}, u32[]{:S(2)}) copy-start(bf16[4,32,8,512]{3,2,1,0:T(8,128)(2,1)S(1)} %get-tuple-element.25) | copy-start | bytes 3145732
  75.5 3.3 %copy-start.4 = (bf16[4,32,8,512]{3,2,1,0:T(8,128)(2,1)}, bf16[4,32,8,512]{3,2,1,0:T(8,128)(2,1)S(1)}, u32[]{:S(2)}) copy-start(bf16[4,32,8,512]{3,2,1,0:T(8,128)(2,1)S(1)} %get-tuple-element.26) | copy-start | bytes 3145732
  85.2 1.2 copy-start.3
  94.2 11.5 %copy-start.1 = (bf16[4,32,8,512]{3,2,1,0:T(8,128)(2,1)S(1)}, bf16[4,32,8,512]{3,2,1,0:T(8,128)(2,1)}, u32[]{:S(2)}) copy-start(bf16[4,32,8,512]{3,2,1,0:T(8,128)(2,1)} %get-tuple-element.27) | copy-start | bytes 3145732
  95.8 36.5 %all-to-all-start.2 = ((bf16[8,16,4096]{2,1,0:T(8,128)(2,1)}), bf16[8,16,4096]{2,1,0:T(8,128)(2,1)S(1)}, u32[]{:S(2)}, u32[]{:S(2)}) async-start(bf16[8,16,4096]{2,1,0:T(8,128)(2,1)} %copy.57), calls=%async_computation.2 | async-start | bytes 2097152 | tf_op jit(solution)/shard_map/all_to_all | solution.py:137
  132.2 30.1 %all-to-all-start.1 = ((bf16[8,16,4096]{2,1,0:T(8,128)(2,1)}), bf16[8,16,4096]{2,1,0:T(8,128)(2,1)S(1)}, u32[]{:S(2)}, u32[]{:S(2)}) async-start(bf16[8,16,4096]{2,1,0:T(8,128)(2,1)} %copy.53), calls=%async_computation.1 | async-start | bytes 2097152 | tf_op jit(solution)/shard_map/all_to_all | solution.py:136
Sparse Core Ops, SparseCore 0:
  9.9 55.3 all-gather.1
  85.4 59.2 reduce-scatter.3
